TPU v7x, 32 devices: a whole 2x2x4 slice. The times are simulated.
32 devices in a mesh: rows: 16 (over z, y, x), heads: 2 (over core).
Axes of the slice: x: 2, y: 2, z: 4, core: 2. Of those that a mesh axis runs over, the one named last changes fastest.
Arguments:
- tokens: bfloat16 [32768, 768], P(('rows', 'heads')), may hold values from -6 to 6
- cotangent: bfloat16 [32768, 768], P(('rows', 'heads')), may hold values from -6 to 6
- segment_ids: int32 [64, 512], P('rows'), may hold values from 0 to 7, never falling along the last dimension, each value on 1 to 256 neighbouring positions
- valid_count: int32 [64], P('rows'), may hold values from 1 to 512, 24576 in all
- qkv_weight: bfloat16 [768, 2304], P(('rows', 'heads')), may hold values from -0.21875 to 0.21875
- qv_bias: bfloat16 [2, 768], P(None, ('rows', 'heads')), may hold values from -0.59765625 to 0.59765625
- out_weight: bfloat16 [768, 768], P(('rows', 'heads')), may hold values from -1.75 to 1.75
- out_bias: bfloat16 [768], P(('rows', 'heads')), may hold values from -1.796875 to 1.796875
- norm_gain: bfloat16 [768], P(('rows', 'heads')), may hold values from 0.5 to 1.5
- norm_shift: bfloat16 [768], P(('rows', 'heads')), may hold values from -1.796875 to 1.796875
- in_weight: bfloat16 [768, 3072], P(('rows', 'heads')), may hold values from -0.21875 to 0.21875
- in_bias: bfloat16 [3072], P(('rows', 'heads')), may hold values from -1.796875 to 1.796875
- back_weight: bfloat16 [3072, 768], P(('rows', 'heads')), may hold values from -0.109375 to 0.109375
- back_bias: bfloat16 [768], P(('rows', 'heads')), may hold values from -1.796875 to 1.796875
- final_gain: bfloat16 [768], P(('rows', 'heads')), may hold values from 0.5 to 1.5
- final_shift: bfloat16 [768], P(('rows', 'heads')), may hold values from -1.796875 to 1.796875
Outputs:
- layer_out: bfloat16 [32768, 768], P(('rows', 'heads'))
- grad_tokens: float32 [32768, 768], P(('rows', 'heads'))
- grad_qkv_weight: float32 [768, 2304], P(('rows', 'heads'))
- grad_qv_bias: float32 [2, 768], P(None, ('rows', 'heads'))
- grad_out_weight: float32 [768, 768], P(('rows', 'heads'))
- grad_out_bias: float32 [768], P(('rows', 'heads'))
- grad_norm_gain: float32 [768], P(('rows', 'heads'))
- grad_norm_shift: float32 [768], P(('rows', 'heads'))
- grad_in_weight: float32 [768, 3072], P(('rows', 'heads'))
- grad_in_bias: float32 [3072], P(('rows', 'heads'))
- grad_back_weight: float32 [3072, 768], P(('rows', 'heads'))
- grad_back_bias: float32 [768], P(('rows', 'heads'))
- grad_final_gain: float32 [768], P(('rows', 'heads'))
- grad_final_shift: float32 [768], P(('rows', 'heads'))
Inputs may be any that keep to these rules, and one draw needn't show every extreme that they name: `segment_ids`: along a row the numbers never fall; each segment spans 1 to 256 positions. `valid_count`: the counts of all 64 rows sum to 24576.
All inputs are finite; a program needn't handle non-finite values. No bound on the sum of `valid_count` on one device may be relied on, other than what follows from the above.
Results may differ from a plain program's by a relative error of at most 0.013.
Values may be sent and summed in bfloat16 or wider, within the bound.
No kernel may reach another device: no remote copies, remote signals or barrier semaphores. Data moves between devices by JAX's collectives and lax.ppermute only.
A program may use at most 192 MiB of HBM per device.

v0:
```python
from functools import partial

import jax
import jax.numpy as jnp
from jax import lax
from jax.sharding import PartitionSpec as P

HEADS = 12
HEAD_DIM = 64


epsilon = 1e-12


def norm_forward(values, gain_row, shift_row):
    centered = values - jnp.mean(values, axis=-1, keepdims=True)
    inverse = lax.rsqrt(jnp.mean(centered * centered, axis=-1, keepdims=True) + epsilon)
    normalized = centered * inverse
    return (normalized * gain_row + shift_row, normalized, inverse)


def norm_backward(grad_output, normalized, inverse, gain_row):
    grad_normed = grad_output * gain_row
    grad_input = inverse * (
        grad_normed
        - jnp.mean(grad_normed, axis=-1, keepdims=True)
        - normalized * jnp.mean(grad_normed * normalized, axis=-1, keepdims=True)
    )
    return (grad_input, jnp.sum(grad_output * normalized, axis=0), jnp.sum(grad_output, axis=0))


def allowed_keys(segment_row, count_row):
    positions = jnp.arange(segment_row.shape[0])
    same_segment = segment_row[:, None] == segment_row[None, :]
    return same_segment & (positions[None, :] < count_row) | (
        positions[:, None] == positions[None, :]
    )


def masked_scores(query_rows, key_rows, allowed):
    scores = jnp.einsum(
        "qhd,khd->hqk", query_rows, key_rows, preferred_element_type=jnp.float32
    ) * HEAD_DIM ** (-0.5)
    return jnp.where(allowed[None], scores, -1e30)


def attend_forward(block_item):
    query_rows, key_rows, value_rows, segment_row, count_row = block_item
    scores = masked_scores(query_rows, key_rows, allowed_keys(segment_row, count_row))
    highest_score = jnp.max(scores, axis=-1, keepdims=True)
    exponent = jnp.exp(scores - highest_score)
    row_total = jnp.sum(exponent, axis=-1, keepdims=True)
    weights_low = (exponent / row_total).astype(jnp.bfloat16)
    context = jnp.einsum(
        "hqk,khd->qhd", weights_low, value_rows, preferred_element_type=jnp.float32
    )
    return (context.astype(jnp.bfloat16), (highest_score + jnp.log(row_total))[..., 0])


def attend_backward(block_item):
    query_rows, key_rows, value_rows, segment_row, count_row, log_total, grad_context = block_item
    scores = masked_scores(query_rows, key_rows, allowed_keys(segment_row, count_row))
    weights_soft = jnp.exp(scores - log_total[..., None])
    weights_low = weights_soft.astype(jnp.bfloat16)
    grad_value = jnp.einsum(
        "hqk,qhd->khd", weights_low, grad_context, preferred_element_type=jnp.float32
    )
    grad_weights = jnp.einsum(
        "qhd,khd->hqk", grad_context, value_rows, preferred_element_type=jnp.float32
    )
    row_inner = jnp.sum(weights_soft * grad_weights, axis=-1, keepdims=True)
    grad_scores = (weights_soft * (grad_weights - row_inner)).astype(jnp.bfloat16)
    scaling = HEAD_DIM ** (-0.5)
    grad_query = (
        jnp.einsum("hqk,khd->qhd", grad_scores, key_rows, preferred_element_type=jnp.float32)
        * scaling
    )
    grad_key = (
        jnp.einsum("hqk,qhd->khd", grad_scores, query_rows, preferred_element_type=jnp.float32)
        * scaling
    )
    return jnp.stack([grad_query, grad_key, grad_value], axis=1).astype(jnp.bfloat16)


def local(
    tokens,
    cotangent,
    segment_ids,
    valid_count,
    qkv_weight,
    qv_bias,
    out_weight,
    out_bias,
    norm_gain,
    norm_shift,
    in_weight,
    in_bias,
    back_weight,
    back_bias,
    final_gain,
    final_shift,
):
    head_count = lax.axis_size("heads")
    head_index = lax.axis_index("heads")
    token_count = tokens.shape[0]
    model_width = tokens.shape[1]
    row_count = segment_ids.shape[0]
    row_length = segment_ids.shape[1]
    local_heads = HEADS // head_count
    local_width = local_heads * HEAD_DIM
    gathered = (
        lax.all_gather(qkv_weight, ("rows", "heads"), axis=0, tiled=True),
        lax.all_gather(qv_bias, ("rows", "heads"), axis=1, tiled=True),
        lax.all_gather(out_weight, ("rows", "heads"), axis=0, tiled=True),
        lax.all_gather(out_bias, ("rows", "heads"), axis=0, tiled=True),
        lax.all_gather(norm_gain, ("rows", "heads"), axis=0, tiled=True),
        lax.all_gather(norm_shift, ("rows", "heads"), axis=0, tiled=True),
        lax.all_gather(in_weight, ("rows", "heads"), axis=0, tiled=True),
        lax.all_gather(in_bias, ("rows", "heads"), axis=0, tiled=True),
        lax.all_gather(back_weight, ("rows", "heads"), axis=0, tiled=True),
        lax.all_gather(back_bias, ("rows", "heads"), axis=0, tiled=True),
        lax.all_gather(final_gain, ("rows", "heads"), axis=0, tiled=True),
        lax.all_gather(final_shift, ("rows", "heads"), axis=0, tiled=True),
    )
    attention_set = gathered[:6]
    feed_set = gathered[6:]
    qkv_all, qv_all, out_all, out_bias_all, gain_all, shift_all = attention_set
    bias_full = jnp.concatenate([qv_all[0], jnp.zeros_like(qv_all[0]), qv_all[1]]).astype(
        jnp.float32
    )
    projected = jnp.dot(tokens, qkv_all, preferred_element_type=jnp.float32) + bias_full
    projected = projected.astype(jnp.bfloat16).reshape(token_count, 3, head_count, local_width)
    arranged = lax.all_to_all(projected, "heads", split_axis=2, concat_axis=0, tiled=True)
    per_row = arranged.reshape(row_count, row_length, 3, local_heads, HEAD_DIM)
    query_all = per_row[:, :, 0]
    key_all = per_row[:, :, 1]
    value_all = per_row[:, :, 2]
    context_local, log_totals = lax.map(
        attend_forward, (query_all, key_all, value_all, segment_ids, valid_count)
    )
    context_send = context_local.reshape(head_count, token_count, local_width)
    context_tokens = lax.all_to_all(
        context_send, "heads", split_axis=0, concat_axis=2, tiled=True
    ).reshape(token_count, model_width)
    flat_index = head_index * token_count + jnp.arange(token_count)
    row_of_token = flat_index // row_length
    position = flat_index % row_length
    row_limit = jnp.sum(
        jnp.where(row_of_token[:, None] == jnp.arange(row_count)[None, :], valid_count[None, :], 0),
        axis=1,
    )
    valid_tokens = (position < row_limit).astype(jnp.float32)[:, None]
    attn = jnp.dot(
        context_tokens, out_all, preferred_element_type=jnp.float32
    ) + out_bias_all.astype(jnp.float32)
    hidden, normed_one, inverse_one = norm_forward(
        tokens.astype(jnp.float32) + attn,
        gain_all.astype(jnp.float32),
        shift_all.astype(jnp.float32),
    )
    hidden_low = hidden.astype(jnp.bfloat16)
    in_all, in_bias_all, back_all, back_bias_all, final_gain_all, final_shift_all = feed_set
    preactive = jnp.dot(
        hidden_low, in_all, preferred_element_type=jnp.float32
    ) + in_bias_all.astype(jnp.float32)
    activation, gelu_pullback = jax.vjp(partial(jax.nn.gelu, approximate=False), preactive)
    activation_low = activation.astype(jnp.bfloat16)
    feed_out = jnp.dot(
        activation_low, back_all, preferred_element_type=jnp.float32
    ) + back_bias_all.astype(jnp.float32)
    final_gain_f = final_gain_all.astype(jnp.float32)
    finished, normed_two, inverse_two = norm_forward(
        hidden + feed_out, final_gain_f, final_shift_all.astype(jnp.float32)
    )
    layer_out = (finished * valid_tokens).astype(jnp.bfloat16)
    grad_final = cotangent.astype(jnp.float32) * valid_tokens
    grad_resid_two, grad_final_gain, grad_final_shift = norm_backward(
        grad_final, normed_two, inverse_two, final_gain_f
    )
    grad_feed = grad_resid_two.astype(jnp.bfloat16)
    grad_back_bias = jnp.sum(grad_feed.astype(jnp.float32), axis=0)
    grad_back_weight = jnp.einsum(
        "tf,td->fd", activation_low, grad_feed, preferred_element_type=jnp.float32
    )
    grad_activation = jnp.einsum(
        "td,fd->tf", grad_feed, back_all, preferred_element_type=jnp.float32
    )
    grad_preactive = gelu_pullback(grad_activation)[0].astype(jnp.bfloat16)
    grad_in_bias = jnp.sum(grad_preactive.astype(jnp.float32), axis=0)
    grad_in_weight = jnp.einsum(
        "td,tf->df", hidden_low, grad_preactive, preferred_element_type=jnp.float32
    )
    grad_hidden = grad_resid_two + jnp.einsum(
        "tf,df->td", grad_preactive, in_all, preferred_element_type=jnp.float32
    )
    grad_resid_one, grad_norm_gain, grad_norm_shift = norm_backward(
        grad_hidden, normed_one, inverse_one, gain_all.astype(jnp.float32)
    )
    grad_attn = grad_resid_one.astype(jnp.bfloat16)
    grad_out_bias = jnp.sum(grad_attn.astype(jnp.float32), axis=0)
    grad_out_weight = jnp.einsum(
        "tc,td->cd", context_tokens, grad_attn, preferred_element_type=jnp.float32
    )
    grad_context = jnp.einsum(
        "td,cd->tc", grad_attn, out_all, preferred_element_type=jnp.float32
    ).astype(jnp.bfloat16)
    grad_context_heads = lax.all_to_all(
        grad_context.reshape(1, token_count, model_width),
        "heads",
        split_axis=2,
        concat_axis=0,
        tiled=True,
    )
    grad_context_rows = grad_context_heads.reshape(row_count, row_length, local_heads, HEAD_DIM)
    grad_arranged = lax.map(
        attend_backward,
        (query_all, key_all, value_all, segment_ids, valid_count, log_totals, grad_context_rows),
    )
    grad_projected = lax.all_to_all(
        grad_arranged.reshape(head_count * token_count, 3, 1, local_width),
        "heads",
        split_axis=0,
        concat_axis=2,
        tiled=True,
    ).reshape(token_count, 3 * model_width)
    grad_qkv_weight = jnp.einsum(
        "td,tc->dc", tokens, grad_projected, preferred_element_type=jnp.float32
    )
    column_sums = jnp.sum(grad_projected.astype(jnp.float32), axis=0).reshape(3, model_width)
    grad_tokens = grad_resid_one + jnp.einsum(
        "tc,dc->td", grad_projected, qkv_all, preferred_element_type=jnp.float32
    )
    grad_qv_bias = jnp.stack([column_sums[0], column_sums[2]])
    summed = (
        lax.psum_scatter(grad_qkv_weight, ("rows", "heads"), scatter_dimension=0, tiled=True),
        lax.psum_scatter(grad_qv_bias, ("rows", "heads"), scatter_dimension=1, tiled=True),
        lax.psum_scatter(grad_out_weight, ("rows", "heads"), scatter_dimension=0, tiled=True),
        lax.psum_scatter(grad_out_bias, ("rows", "heads"), scatter_dimension=0, tiled=True),
        lax.psum_scatter(grad_norm_gain, ("rows", "heads"), scatter_dimension=0, tiled=True),
        lax.psum_scatter(grad_norm_shift, ("rows", "heads"), scatter_dimension=0, tiled=True),
        lax.psum_scatter(grad_in_weight, ("rows", "heads"), scatter_dimension=0, tiled=True),
        lax.psum_scatter(grad_in_bias, ("rows", "heads"), scatter_dimension=0, tiled=True),
        lax.psum_scatter(grad_back_weight, ("rows", "heads"), scatter_dimension=0, tiled=True),
        lax.psum_scatter(grad_back_bias, ("rows", "heads"), scatter_dimension=0, tiled=True),
        lax.psum_scatter(grad_final_gain, ("rows", "heads"), scatter_dimension=0, tiled=True),
        lax.psum_scatter(grad_final_shift, ("rows", "heads"), scatter_dimension=0, tiled=True),
    )
    return (layer_out, grad_tokens) + tuple(summed)


def solution(mesh):
    in_specs = (
        P(("rows", "heads"), None),
        P(("rows", "heads"), None),
        P("rows", None),
        P("rows"),
        P(("rows", "heads"), None),
        P(None, ("rows", "heads")),
        P(("rows", "heads"), None),
        P(("rows", "heads")),
        P(("rows", "heads")),
        P(("rows", "heads")),
        P(("rows", "heads"), None),
        P(("rows", "heads")),
        P(("rows", "heads"), None),
        P(("rows", "heads")),
        P(("rows", "heads")),
        P(("rows", "heads")),
    )
    out_specs = (
        P(("rows", "heads"), None),
        P(("rows", "heads"), None),
        P(("rows", "heads"), None),
        P(None, ("rows", "heads")),
        P(("rows", "heads"), None),
        P(("rows", "heads")),
        P(("rows", "heads")),
        P(("rows", "heads")),
        P(("rows", "heads"), None),
        P(("rows", "heads")),
        P(("rows", "heads"), None),
        P(("rows", "heads")),
        P(("rows", "heads")),
        P(("rows", "heads")),
    )
    return jax.shard_map(local, mesh=mesh, in_specs=in_specs, out_specs=out_specs, check_vma=False)
```

profile of v0, /device:TPU:0, one launch (start us, length us, event | category | flops | bytes accessed | tf_op | source)
XLA Modules:
  0.0 907.3 jit_solution(11968919574420421245)
XLA Ops:
  15.9 42.6 %all-reduce.16 = (bf16[768]{0:T(1024)(128)(2,1)S(1)}, bf16[768]{0:T(1024)(128)(2,1)S(1)}, bf16[768]{0:T(1024)(128)(2,1)S(1)}, bf16[3072]{0:T(1024)(128)(2,1)S(1)...) all-reduce(bf16[768]{0:T(1024)(128)(2,1)S(1)} %dynamic-update-slice, ...), channel_id=1, replica_groups=mesh['rows'=16,'heads'=2] {'rows','heads'}, use_global_device_ids=true, to_apply=%add | all-reduce | flops 7680 | bytes 30720
  58.5 40.2 %all-gather = bf16[32,24,2]{1,2,0:T(2,128)(2,1)S(1)} all-gather(bf16[1,24,2]{1,2,0:T(2,128)(2,1)} %bitcast.190), channel_id=1, replica_groups=mesh['rows'=16,'heads'=2] {'rows','heads'}, dimensions={0}, use_global_device_ids=true | all-gather | bytes 3168 | tf_op jit(solution)/shard_map/all_gather | solution.py:113
  113.3 9.9 %reshape.371 = bf16[1024,3,2,384]{3,2,1,0:T(2,128)(2,1)} reshape(bf16[1024,2304]{1,0:T(8,128)(2,1)} %add_convert_fusion.1) | data formatting | bytes 9437184 | tf_op jit(solution)/shard_map/reshape | solution.py:132
  123.2 12.5 %copy.135 = bf16[1024,3,2,384]{0,3,1,2:T(8,128)(2,1)} copy(bf16[1024,3,2,384]{3,2,1,0:T(2,128)(2,1)} %reshape.371) | data formatting | bytes 9437184 | tf_op jit(solution)/shard_map/reshape | solution.py:132
  135.7 12.9 %all_to_all.60 = bf16[1024,3,2,384]{0,3,1,2:T(8,128)(2,1)} all-to-all(bf16[1024,3,2,384]{0,3,1,2:T(8,128)(2,1)} %copy.135), channel_id=1, replica_groups=mesh['rows'=16,'heads'=2] {'heads'}, dimensions={2} | all-to-all | bytes 9437184 | tf_op jit(solution)/shard_map/all_to_all | solution.py:133
  148.6 9.4 %copy.136 = bf16[2,1024,3,1,384]{1,0,4,2,3:T(2,128)(2,1)} copy(bf16[2,1024,3,1,384]{1,4,2,0,3:T(8,128)(2,1)} %bitcast.179) | data formatting | bytes 9437184 | tf_op jit(solution)/shard_map/all_to_all | solution.py:133
  157.9 12.0 %reshape.372 = bf16[4,512,3,6,64]{1,0,4,3,2:T(4,128)(2,1)} reshape(bf16[2,1024,3,1,384]{1,0,4,2,3:T(2,128)(2,1)} %copy.136) | data formatting | bytes 9437184 | tf_op jit(solution)/shard_map/reshape | solution.py:134
  175.9 36.5 %while.22 = (s32[]{:T(128)}, bf16[4,512,6,64]{1,3,2,0:T(8,128)(2,1)}, f32[4,6,512]{2,1,0:T(8,128)}, bf16[4,512,6,64]{1,3,2,0:T(8,128)(2,1)}, s32[4,512]{1,0:T(4,...) while((s32[]{:T(128)}, ...), condition=%wide.region_3.4_spmd, body=%wide.region_0.3_spmd.sunk | while | flops 422770176 | bytes 21608048 | solution.py:138
  238.2 39.1 %multiply_convert_fusion.1 = (bf16[1024,3072]{1,0:T(8,128)(2,1)}, f32[1024,3072]{1,0:T(8,128)}, f32[1024,3072]{1,0:T(8,128)}) fusion(f32[3072]{0:T(1024)S(1)} %convert_element_type.109, bf16[768,3072]{1,0:T(8,128)(2,1)} %all-gather.10.cloned.1.call-done, f32[1024,768]{0,1:T(8,128)} %copy-done.4, f32[768]{0:T(1024)S(1)} %convert_element_type.107, ...), kind=kOutput, calls=%fused_computation.72 | convolution fusion | flops 5043388416 | bytes 39348224 | tf_op jit(solution)/shard_map/dot_general | solution.py:163
  277.3 9.1 %fusion.85 = (f32[1024]{0:T(1024)S(1)}, f32[1024,768]{0,1:T(8,128)S(1)}) fusion(f32[768]{0:T(1024)S(1)} %copy-done.28, bf16[1024,3072]{1,0:T(8,128)(2,1)} %get-tuple-element.308, bf16[3072,768]{1,0:T(8,128)(2,1)} %all-gather.12.cloned.1.call-done, f32[768]{0:T(1024)S(1)} %convert_element_type.107, f32[768]{0:T(1024)S(1)} %convert_element_type.106, ...), kind=kOutput, calls=%fused_computation.156 | convolution fusion | flops 4837342208 | bytes 17323008 | tf_op jit(solution)/shard_map/dot_general | solution.py:168
  293.3 18.1 %convert_reduce_fusion = (f32[3072]{0:T(1024)}, bf16[1024,3072]{1,0:T(8,128)(2,1)}) fusion(f32[1024,3072]{1,0:T(8,128)} %get-tuple-element.309, bf16[1024,768]{0,1:T(8,128)(2,1)S(1)} %get-tuple-element.305, bf16[3072,768]{1,0:T(8,128)(2,1)} %all-gather.12.cloned.1.call-done, f32[1024,3072]{1,0:T(8,128)} %get-tuple-element.322, ...), kind=kOutput, calls=%fused_computation.70 | convolution fusion | flops 4885312512 | bytes 37773312 | tf_op jit(solution)/shard_map/td,fd->tf/dot_general | solution.py:185
  311.5 12.1 %multiply_reduce_fusion.2 = (f32[768]{0:T(1024)}, f32[1024]{0:T(1024)S(1)}, f32[1024]{0:T(1024)S(1)}, f32[768]{0:T(1024)}, f32[1024,768]{0,1:T(8,128)S(1)}) fusion(f32[1024,768]{0,1:T(8,128)} %copy-done.4, f32[1024]{0:T(1024)S(1)} %add_rsqrt_fusion.1, f32[1024]{0:T(1024)S(1)} %broadcast_multiply_fusion.5, f32[768]{0:T(1024)S(1)} %convert_element_type.106, ...), kind=kOutput, calls=%fused_computation.91 | convolution fusion | flops 4846776320 | bytes 22069248 | tf_op jit(solution)/shard_map/tf,df->td/dot_general | solution.py:193
  341.4 11.0 %reduce.6 = bf16[768,1024]{1,0:T(8,128)(2,1)} reduce(bf16[768,1,1024]{2,1,0:T(2,128)(2,1)S(1)} %bitcast.180, bf16[]{:T(256)} %broadcast.301), dimensions={1}, to_apply=%bitcast.101.reduce_sub_computation | reduce | bytes 3145730
  369.3 67.7 %while.23 = (s32[]{:T(128)}, bf16[4,512,3,6,64]{1,4,3,2,0:T(8,128)(2,1)}, bf16[4,512,6,64]{1,3,2,0:T(8,128)(2,1)}, s32[4,512]{1,0:T(4,128)}, s32[4]{0:T(128)S(1)...) while((s32[]{:T(128)}, ...), condition=%wide.region_15.16_spmd, body=%wide.region_13.15_spmd.sunk | while | flops 1035793920 | bytes 67209912 | solution.py:215
  445.5 9.0 reshape.377
  454.5 10.3 %copy.152 = bf16[2048,3,1,384]{3,1,2,0:T(4,128)(2,1)} copy(bf16[2048,3,1,384]{0,3,1,2:T(8,128)(2,1)} %reshape.377) | data formatting | bytes 9437184 | tf_op jit(solution)/shard_map/reshape | solution.py:220
  464.8 10.3 %all_to_all.62 = bf16[2048,3,1,384]{3,1,2,0:T(4,128)(2,1)S(1)} all-to-all(bf16[2048,3,1,384]{3,1,2,0:T(4,128)(2,1)} %copy.152), channel_id=1, replica_groups=mesh['rows'=16,'heads'=2] {'heads'}, dimensions={0} | all-to-all | bytes 9437184 | tf_op jit(solution)/shard_map/all_to_all | solution.py:219
  502.9 10.7 %fusion.78 = f32[768,3072]{1,0:T(8,128)} fusion(bf16[1024,3072]{1,0:T(8,128)(2,1)} %get-tuple-element.327, f32[1024,768]{0,1:T(8,128)S(1)} %copy-done.7, f32[768]{0:T(1024)S(1)} %copy-done.27, f32[768]{0:T(1024)S(1)} %convert_element_type.106, f32[1024]{0:T(1024)S(1)} %add_rsqrt_fusion.1, f32[1024]{0:T(1024)S(1)} %broadcast_multiply_fusion.5), kind=kOutput, calls=%fused_computation.153 | convolution fusion | flops 4835770368 | bytes 18888704 | tf_op jit(solution)/shard_map/td,tf->df/dot_general | solution.py:190
  515.1 10.4 %fusion.86 = f32[3072,768]{1,0:T(8,128)} fusion(bf16[1024,3072]{1,0:T(8,128)(2,1)} %get-tuple-element.308, bf16[1024,768]{0,1:T(8,128)(2,1)S(1)} %copy-done.18), kind=kOutput, calls=%fused_computation.157 | convolution fusion | flops 4831838208 | bytes 17301504 | tf_op jit(solution)/shard_map/tf,td->fd/dot_general | solution.py:182
  528.9 39.1 %all-reduce.15 = (f32[2,768]{1,0:T(2,128)S(1)}, f32[768]{0:T(1024)S(1)}, f32[768]{0:T(1024)S(1)}, f32[768]{0:T(1024)S(1)}, f32[3072]{0:T(1024)S(1)}, /*index=5*/...) all-reduce(f32[2,768]{1,0:T(2,128)S(1)} %pad_maximum_fusion, ...), channel_id=3, replica_groups=mesh['rows'=16,'heads'=2] {'rows','heads'}, use_global_device_ids=true, to_apply=%region_18.19.clone | all-reduce | flops 9216 | bytes 73728
  571.6 8.9 convolution_add_fusion.1
  587.0 29.7 %reduce-scatter.14.cloned.1.call-done = f32[24,2304]{1,0:T(8,128)} async-done(((f32[768,2304]{1,0:T(8,128)}), f32[24,2304]{1,0:T(8,128)}) %reduce-scatter.14.cloned.1.call-update) | async-done | bytes 221200
  616.7 141.6 %reduce-scatter.10.cloned.1.call-done = f32[24,3072]{1,0:T(8,128)} async-done(((f32[768,3072]{1,0:T(8,128)}), f32[24,3072]{1,0:T(8,128)}) %reduce-scatter.10.cloned.1.call-update) | async-done | bytes 294928 | tf_op jit(solution)/shard_map/reduce_scatter | solution.py:241
  758.3 141.9 %reduce-scatter.12.cloned.1.call-done = f32[96,768]{1,0:T(8,128)} async-done(((f32[3072,768]{1,0:T(8,128)}), f32[96,768]{1,0:T(8,128)}) %reduce-scatter.12.cloned.1.call-update) | async-done | bytes 294928 | tf_op jit(solution)/shard_map/reduce_scatter | solution.py:243
  (267 shorter events, 251.0 us)
Async XLA Ops:
  7.2 95.6 %copy-start.31 = (s32[4]{0:T(128)S(1)}, s32[4]{0:T(128)}, u32[]{:S(2)}) copy-start(s32[4]{0:T(128)} %param.23) | copy-start | bytes 52
  7.2 96.3 %copy-start.13 = (bf16[1024,768]{1,0:T(8,128)(2,1)S(1)}, bf16[1024,768]{1,0:T(8,128)(2,1)}, u32[]{:S(2)}) copy-start(bf16[1024,768]{1,0:T(8,128)(2,1)} %param.21) | copy-start | bytes 4718596
  7.2 98.6 %all-gather.6.cloned.1.call-start = ((), (), s32[]{:S(2)}) async-start(), calls=%async_computation.8 | async-start | bytes 3649536 | tf_op jit(solution)/shard_map/all_gather | solution.py:112
  7.9 222.2 %all-gather.8.cloned.1.call-start = ((), (), s32[]{:S(2)}) async-start(), calls=%async_computation.9 | async-start | bytes 1216512 | tf_op jit(solution)/shard_map/all_gather | solution.py:114
  8.7 229.5 %all-gather.10.cloned.1.call-start = ((), (), s32[]{:S(2)}) async-start(), calls=%async_computation.10 | async-start | bytes 4866048 | tf_op jit(solution)/shard_map/all_gather | solution.py:118
  9.4 267.8 %all-gather.12.cloned.1.call-start = ((), (), s32[]{:S(2)}) async-start(), calls=%async_computation.11 | async-start | bytes 4866048 | tf_op jit(solution)/shard_map/all_gather | solution.py:120
  98.9 6.9 copy-start.14
  101.6 175.7 %copy-start.26 = (f32[768]{0:T(1024)}, f32[768]{0:T(1024)S(1)}, u32[]{:S(2)}) copy-start(f32[768]{0:T(1024)S(1)} %convert_element_type.107) | copy-start | bytes 9220
  212.4 9.9 %copy-start = (bf16[4,512,6,64]{1,3,2,0:T(8,128)(2,1)}, bf16[4,512,6,64]{1,3,2,0:T(8,128)(2,1)S(1)}, u32[]{:S(2)}) copy-start(bf16[4,512,6,64]{1,3,2,0:T(8,128)(2,1)S(1)} %get-tuple-element.507) | copy-start | bytes 4718596
  212.4 23.7 %copy-start.2 = (bf16[4,512,6,64]{1,3,2,0:T(8,128)(2,1)}, bf16[4,512,6,64]{1,3,2,0:T(8,128)(2,1)S(1)}, u32[]{:S(2)}) copy-start(bf16[4,512,6,64]{1,3,2,0:T(8,128)(2,1)S(1)} %get-tuple-element.508) | copy-start | bytes 4718596
  225.3 7.4 copy-start.16
  225.3 7.4 all-to-all-start.1
  230.1 356.9 %reduce-scatter.8.cloned.1.call-start = ((), (), s32[]{:S(2)}) async-start(), calls=%async_computation.12 | async-start | bytes 2433024 | tf_op jit(solution)/shard_map/reduce_scatter | solution.py:237
  238.1 39.1 %copy-start.5 = (f32[1024,768]{0,1:T(8,128)S(1)}, f32[1024,768]{0,1:T(8,128)}, u32[]{:S(2)}) copy-start(f32[1024,768]{0,1:T(8,128)} %copy-done.4) | copy-start | bytes 9437188
  238.2 39.1 %copy-start.28 = (f32[768]{0:T(1024)S(1)}, f32[768]{0:T(1024)}, u32[]{:S(2)}) copy-start(f32[768]{0:T(1024)} %convert_element_type.111) | copy-start | bytes 9220
  293.3 18.1 %copy-start.17 = (bf16[1024,768]{0,1:T(8,128)(2,1)}, bf16[1024,768]{0,1:T(8,128)(2,1)S(1)}, u32[]{:S(2)}) copy-start(bf16[1024,768]{0,1:T(8,128)(2,1)S(1)} %get-tuple-element.305) | copy-start | bytes 4718596
  311.5 12.1 %copy-start.6 = (f32[1024,768]{0,1:T(8,128)S(1)}, f32[1024,768]{0,1:T(8,128)}, u32[]{:S(2)}) copy-start(f32[1024,768]{0,1:T(8,128)} %copy-done.4) | copy-start | bytes 9437188
  324.6 5.3 copy-start.11
  369.2 247.5 %reduce-scatter.14.cloned.1.call-start = ((), (), s32[]{:S(2)}) async-start(), calls=%async_computation.15 | async-start | bytes 7299072
  369.3 5.0 copy-start.8
  478.0 6.8 copy-start.15
  500.9 257.4 %reduce-scatter.10.cloned.1.call-start = ((), (), s32[]{:S(2)}) async-start(), calls=%async_computation.13 | async-start | bytes 9732096 | tf_op jit(solution)/shard_map/reduce_scatter | solution.py:241
  513.6 386.6 %reduce-scatter.12.cloned.1.call-start = ((), (), s32[]{:S(2)}) async-start(), calls=%async_computation.14 | async-start | bytes 9732096 | tf_op jit(solution)/shard_map/reduce_scatter | solution.py:243
  525.5 46.1 %copy-start.12 = (f32[1024,768]{0,1:T(8,128)S(1)}, f32[1024,768]{0,1:T(8,128)}, u32[]{:S(2)}) copy-start(f32[1024,768]{0,1:T(8,128)} %copy-done.11) | copy-start | bytes 9437188
  (24 other events, 73.6 us)
Sparse Core Ops, SparseCore 0:
  10.9 62.6 all-gather.5
  76.5 52.7 all-gather.7
  132.2 62.4 all-gather.9
  197.5 61.9 all-gather.11
  369.3 95.5 reduce-scatter.7
  501.0 115.6 reduce-scatter.13
  623.1 135.0 reduce-scatter.9
  764.8 135.3 reduce-scatter.11
where the time goes:
time: 916 us; the launch traced here: 907 us
  waiting for transfers between devices  318 us (35%)
  matrix products  200 us (22%)
  local copies, waits for them, and re-layouts  166 us (18%)
  blocking collectives  151 us (16%)
  other arithmetic  51.5 us (6%)
  between operations  15 us (2%)
    reduce_scatter x1, waiting for transfers between devices, local(): lax.psum_scatter(grad_back_weight, ('rows', 'heads'), scatter_dimension=0...  142 us
    reduce_scatter x1, waiting for transfers between devices, local(): lax.psum_scatter(grad_in_weight, ('rows', 'heads'), scatter_dimension=0,...  142 us
    unnamed x2, blocking collectives  81.7 us
    all_gather x1, blocking collectives, local(): lax.all_gather(qv_bias, ('rows', 'heads'), axis=1, tiled=True)  40.2 us
    unnamed x91, local copies, waits for them, and re-layouts  40.2 us
    dot_general x1, matrix products, local(): jnp.dot(hidden_low, in_all, preferred_element_type=jnp.float32)  39.1 us
    unnamed x9, waiting for transfers between devices  32.4 us
    reshape x2, local copies, waits for them, and re-layouts, local(): projected.astype(jnp.bfloat16)  22.4 us
  transfers between devices with their start and end apart: 9, of which 4 were waited for; matrix products, arithmetic and copies ran while one was open for 36% of the time, Pallas kernels for 0%

commit v1 on v0

v1 whole, which is shorter than its diff:
```python
import math

import jax
import jax.numpy as jnp
from jax import lax
from jax.sharding import PartitionSpec as P

HEADS = 12
HEAD_DIM = 64
EPS = 1e-12
AXES = ("rows", "heads")
F32 = jnp.float32
BF16 = jnp.bfloat16


def norm_forward(values, gain_row, shift_row):
    centered = values - jnp.mean(values, axis=-1, keepdims=True)
    inverse = lax.rsqrt(jnp.mean(centered * centered, axis=-1, keepdims=True) + EPS)
    normalized = centered * inverse
    return (normalized * gain_row + shift_row, normalized, inverse)


def norm_backward(grad_output, normalized, inverse, gain_row):
    grad_normed = grad_output * gain_row
    grad_input = inverse * (
        grad_normed
        - jnp.mean(grad_normed, axis=-1, keepdims=True)
        - normalized * jnp.mean(grad_normed * normalized, axis=-1, keepdims=True)
    )
    return (grad_input, jnp.sum(grad_output * normalized, axis=0), jnp.sum(grad_output, axis=0))


def allowed_keys(segment_row, count_row):
    positions = jnp.arange(segment_row.shape[0])
    same_segment = segment_row[:, None] == segment_row[None, :]
    return same_segment & (positions[None, :] < count_row) | (
        positions[:, None] == positions[None, :]
    )


def masked_scores(query_rows, key_rows, allowed):
    scores = jnp.einsum(
        "qhd,khd->hqk", query_rows, key_rows, preferred_element_type=F32
    ) * HEAD_DIM ** (-0.5)
    return jnp.where(allowed[None], scores, -1e30)


def attend_forward(query_rows, key_rows, value_rows, segment_row, count_row):
    scores = masked_scores(query_rows, key_rows, allowed_keys(segment_row, count_row))
    highest = jnp.max(scores, axis=-1, keepdims=True)
    exponent = jnp.exp(scores - highest)
    total = jnp.sum(exponent, axis=-1, keepdims=True)
    low = (exponent / total).astype(BF16)
    context = jnp.einsum("hqk,khd->qhd", low, value_rows, preferred_element_type=F32)
    return (context.astype(BF16), (highest + jnp.log(total))[..., 0])


def attend_backward(query_rows, key_rows, value_rows, segment_row, count_row, lse, grad_context):
    scores = masked_scores(query_rows, key_rows, allowed_keys(segment_row, count_row))
    soft = jnp.exp(scores - lse[..., None])
    low = soft.astype(BF16)
    grad_value = jnp.einsum("hqk,qhd->khd", low, grad_context, preferred_element_type=F32)
    grad_soft = jnp.einsum("qhd,khd->hqk", grad_context, value_rows, preferred_element_type=F32)
    inner = jnp.sum(soft * grad_soft, axis=-1, keepdims=True)
    grad_scores = (soft * (grad_soft - inner)).astype(BF16)
    scaling = HEAD_DIM ** (-0.5)
    grad_query = (
        jnp.einsum("hqk,khd->qhd", grad_scores, key_rows, preferred_element_type=F32) * scaling
    )
    grad_key = (
        jnp.einsum("hqk,qhd->khd", grad_scores, query_rows, preferred_element_type=F32) * scaling
    )
    return tuple(g.astype(BF16) for g in (grad_query, grad_key, grad_value))


def local(
    tokens, cotangent, segment_ids, valid_count, qkv_weight, qv_bias, out_weight, out_bias,
    norm_gain, norm_shift, in_weight, in_bias, back_weight, back_bias, final_gain, final_shift,
):
    head_index = lax.axis_index("heads")
    devices = lax.axis_size("rows") * lax.axis_size("heads")
    token_count, width = tokens.shape
    row_length = segment_ids.shape[1]
    rows = token_count // row_length
    shard = qkv_weight.shape[0]
    small = [qv_bias[0], qv_bias[1], out_bias, norm_gain, norm_shift, in_bias, back_bias,
             final_gain, final_shift]
    sizes = [s.shape[0] for s in small]
    total = sum(sizes)
    lanes = -(-total // (shard * 128)) * 128
    packed = jnp.pad(jnp.concatenate(small), (0, shard * lanes - total)).reshape(shard, lanes)
    first = lax.all_gather(
        jnp.concatenate([qkv_weight, packed], axis=1), AXES, axis=0, tiled=True
    )
    qkv_all = first[:, : 3 * width]
    vectors = first[:, 3 * width :].reshape(devices, shard * lanes)
    parts = []
    at = 0
    for n in sizes:
        parts.append(vectors[:, at : at + n].reshape(devices * n).astype(F32))
        at += n
    (q_bias, v_bias, out_bias_f, gain_f, shift_f, in_bias_f, back_bias_f, fgain_f, fshift_f) = parts
    second = lax.all_gather(
        jnp.concatenate([out_weight, in_weight], axis=1), AXES, axis=0, tiled=True
    )
    out_all = second[:, :width]
    in_all = second[:, width:]
    back_all = lax.all_gather(back_weight, AXES, axis=0, tiled=True)

    segments = lax.dynamic_slice(segment_ids, (head_index * rows, 0), (rows, row_length))
    counts = lax.dynamic_slice(valid_count, (head_index * rows,), (rows,))
    bias_full = jnp.concatenate([q_bias, jnp.zeros_like(q_bias), v_bias])
    projected = (jnp.dot(tokens, qkv_all, preferred_element_type=F32) + bias_full).astype(BF16)
    heads = projected.reshape(rows, row_length, 3, HEADS, HEAD_DIM)
    contexts = [
        attend_forward(heads[r, :, 0], heads[r, :, 1], heads[r, :, 2], segments[r], counts[r])
        for r in range(rows)
    ]
    context = jnp.concatenate([c[0].reshape(row_length, width) for c in contexts], axis=0)
    valid = (
        (jnp.arange(row_length)[None, :] < counts[:, None]).astype(F32).reshape(token_count, 1)
    )
    attn = jnp.dot(context, out_all, preferred_element_type=F32) + out_bias_f
    hidden, n1, r1 = norm_forward(tokens.astype(F32) + attn, gain_f, shift_f)
    hidden_low = hidden.astype(BF16)
    preact = jnp.dot(hidden_low, in_all, preferred_element_type=F32) + in_bias_f
    cdf = 0.5 + 0.5 * lax.erf(preact * (0.5 ** 0.5))
    activation = (preact * cdf).astype(BF16)
    slope = (cdf + preact * jnp.exp(-0.5 * preact * preact) * (1.0 / math.sqrt(2 * math.pi))).astype(BF16)
    feed = jnp.dot(activation, back_all, preferred_element_type=F32) + back_bias_f
    finished, n2, r2 = norm_forward(hidden + feed, fgain_f, fshift_f)
    layer_out = (finished * valid).astype(BF16)
    grad_final = cotangent.astype(F32) * valid
    g_res2, g_fgain, g_fshift = norm_backward(grad_final, n2, r2, fgain_f)
    g_ffn = g_res2.astype(BF16)
    g_back_bias = jnp.sum(g_ffn.astype(F32), axis=0)
    g_back = jnp.einsum("tf,td->fd", activation, g_ffn, preferred_element_type=F32).astype(BF16)
    g_back = lax.psum_scatter(g_back, AXES, scatter_dimension=0, tiled=True)
    g_act = jnp.einsum("td,fd->tf", g_ffn, back_all, preferred_element_type=F32)
    g_pre = (g_act * slope.astype(F32)).astype(BF16)
    g_in_bias = jnp.sum(g_pre.astype(F32), axis=0)
    g_in = jnp.einsum("td,tf->df", hidden_low, g_pre, preferred_element_type=F32).astype(BF16)
    g_hidden = g_res2 + jnp.einsum("tf,df->td", g_pre, in_all, preferred_element_type=F32)
    g_res1, g_gain, g_shift = norm_backward(g_hidden, n1, r1, gain_f)
    g_attn = g_res1.astype(BF16)
    g_out_bias = jnp.sum(g_attn.astype(F32), axis=0)
    g_out = jnp.einsum("tc,td->cd", context, g_attn, preferred_element_type=F32).astype(BF16)
    g_oi = lax.psum_scatter(
        jnp.concatenate([g_out, g_in], axis=1), AXES, scatter_dimension=0, tiled=True
    )
    g_context = jnp.einsum("td,cd->tc", g_attn, out_all, preferred_element_type=F32).astype(BF16)
    g_heads = g_context.reshape(rows, row_length, HEADS, HEAD_DIM)
    grads = [
        attend_backward(heads[r, :, 0], heads[r, :, 1], heads[r, :, 2], segments[r], counts[r],
                        contexts[r][1], g_heads[r])
        for r in range(rows)
    ]
    g_proj = jnp.concatenate(
        [jnp.concatenate([g.reshape(row_length, width) for g in row], axis=1) for row in grads],
        axis=0,
    )
    g_qkv = jnp.einsum("td,tc->dc", tokens, g_proj, preferred_element_type=F32).astype(BF16)
    sums = jnp.sum(g_proj.astype(F32), axis=0).reshape(3, width)
    g_small = [sums[0], sums[2], g_out_bias, g_gain, g_shift, g_in_bias, g_back_bias, g_fgain,
               g_fshift]
    g_packed = jnp.concatenate([g.reshape(devices, -1) for g in g_small], axis=1)
    g_packed = jnp.pad(g_packed, ((0, 0), (0, shard * lanes - total))).astype(BF16)
    g_last = lax.psum_scatter(
        jnp.concatenate([g_qkv, g_packed.reshape(devices * shard, lanes)], axis=1),
        AXES, scatter_dimension=0, tiled=True,
    )
    grad_tokens = g_res1 + jnp.einsum("tc,dc->td", g_proj, qkv_all, preferred_element_type=F32)
    mine = g_last[:, 3 * width :].reshape(shard * lanes).astype(F32)
    own = []
    at = 0
    for n in sizes:
        own.append(mine[at : at + n])
        at += n
    return (
        layer_out, grad_tokens, g_last[:, : 3 * width].astype(F32), jnp.stack([own[0], own[1]]),
        g_oi[:, :width].astype(F32), own[2], own[3], own[4], g_oi[:, width:].astype(F32), own[5],
        g_back.astype(F32), own[6], own[7], own[8],
    )


def solution(mesh):
    both = P(AXES, None)
    vec = P(AXES)
    in_specs = (both, both, P("rows", None), P("rows"), both, P(None, AXES), both, vec, vec, vec,
                both, vec, both, vec, vec, vec)
    out_specs = (both, both, both, P(None, AXES), both, vec, vec, vec, both, vec, both, vec, vec,
                 vec)
    return jax.shard_map(local, mesh=mesh, in_specs=in_specs, out_specs=out_specs, check_vma=False)
```

time: 916 us -> 749 us (0.82)
  blocking collectives: 151 us -> 0 us
  waiting for transfers between devices: 318 us -> 425 us
  local copies, waits for them, and re-layouts: 166 us -> 67.8 us
  matrix products: 200 us -> 176 us
    all_gather x4 -> x3, waiting for transfers between devices: 0.06 us -> 107 us  [the longest x1 54.4 us: local(): lax.all_gather(jnp.concatenate([qkv_weight, packed], axis=1), AXES, axis=...]
    unnamed x2 -> x0, blocking collectives: 81.7 us -> none
    unnamed x9 -> x7, waiting for transfers between devices: 32.4 us -> 95.5 us
    reduce_scatter x3 -> x2, waiting for transfers between devices: 284 us -> 223 us  [the longest x1 116 us: local(): lax.psum_scatter(jnp.concatenate([g_out, g_in], axis=1), AXES, scatter_di...]
    reshape x9 -> x12, local copies, waits for them, and re-layouts: 70.5 us -> 21.2 us  [the longest x7 8.88 us: local(): g.reshape(devices, -1)]
    all_gather x1 -> x0, blocking collectives: 40.2 us -> none  [local(): lax.all_gather(qv_bias, ('rows', 'heads'), axis=1, tiled=True)]
    all_to_all x3 -> x0, blocking collectives: 29.2 us -> none  [the longest x1 12.9 us: local(): lax.all_to_all(projected, 'heads', split_axis=2, concat_axis=0, tiled=True)]
    unnamed x91 -> x95, local copies, waits for them, and re-layouts: 40.2 us -> 14.7 us
  transfers between devices with their start and end apart: 9 -> 6, of which waited for: 4 -> 6; matrix products, arithmetic and copies ran while one was open for 36% -> 18% of each run, Pallas kernels for 0% -> 0%
where the time goes in v1:
time: 749 us; the launch traced here: 741 us
  waiting for transfers between devices  425 us (57%)
  matrix products  176 us (23%)
  local copies, waits for them, and re-layouts  67.8 us (9%)
  other arithmetic  56.3 us (8%)
  between operations  15.3 us (2%)
    reduce_scatter x1, waiting for transfers between devices, local(): lax.psum_scatter(jnp.concatenate([g_out, g_in], axis=1), AXES, scatter_di...  116 us
    reduce_scatter x1, waiting for transfers between devices, local(): g_back = lax.psum_scatter(g_back, AXES, scatter_dimension=0, tiled=True)  107 us
    unnamed x7, waiting for transfers between devices  95.5 us
    all_gather x1, waiting for transfers between devices, local(): lax.all_gather(jnp.concatenate([qkv_weight, packed], axis=1), AXES, axis=...  54.4 us
    all_gather x1, waiting for transfers between devices, local(): back_all = lax.all_gather(back_weight, AXES, axis=0, tiled=True)  48.5 us
    dot_general x1, matrix products, local(): jnp.einsum('td,tc->dc', tokens, g_proj, preferred_element_type=F32)  28.5 us
    convert_element_type x2, other arithmetic, attend_backward(): grad_scores = (soft * (grad_soft - inner)).astype(BF16)  17.1 us
    dot_general x1, matrix products, local(): g_act = jnp.einsum('td,fd->tf', g_ffn, back_all, preferred_element_type=F32)  16.2 us
  transfers between devices with their start and end apart: 6, of which 6 were waited for; matrix products, arithmetic and copies ran while one was open for 18% of the time, Pallas kernels for 0%

profile of v1, /device:TPU:0, one launch (start us, length us, event | category | flops | bytes accessed | tf_op | source)
XLA Modules:
  0.0 740.6 jit_solution(17252090711581574381)
XLA Ops:
  23.5 54.4 %all-gather.4.cloned.1.call-done = bf16[768,2432]{1,0:T(8,128)(2,1)} async-done(((bf16[24,2432]{1,0:T(8,128)(2,1)}), bf16[768,2432]{1,0:T(8,128)(2,1)}) %all-gather.4.cloned.1.call-update) | async-done | bytes 3735568 | tf_op jit(solution)/shard_map/all_gather | solution.py:92
  79.2 9.0 %fusion.17 = bf16[1024,2304]{0,1:T(8,128)(2,1)} fusion(bf16[1024,768]{1,0:T(8,128)(2,1)} %param.16, f32[2304]{0:T(1024)S(1)} %pad_maximum_fusion.7, bf16[768,2432]{1,0:T(8,128)(2,1)} %all-gather.4.cloned.1.call-done), kind=kOutput, calls=%fused_computation.36 | convolution fusion | flops 3628597248 | bytes 9839616 | tf_op jit(solution)/shard_map/dot_general | solution.py:113
  88.2 8.8 %reshape.390 = bf16[2,512,3,12,64]{1,0,4,3,2:T(2,128)(2,1)} reshape(bf16[1024,2304]{0,1:T(8,128)(2,1)} %fusion.17) | data formatting | bytes 9437184 | tf_op jit(solution)/shard_map/reshape | solution.py:114
  97.1 12.3 %fusion.72 = (bf16[1,512,1,12,64]{1,0,4,3,2:T(2,128)(2,1)}, bf16[1,512,1,12,64]{1,0,4,3,2:T(2,128)(2,1)S(1)}, bf16[1,512,1,12,64]{1,0,4,3,2:T(2,128)(2,1)}, bf16...) fusion(bf16[2,512,3,12,64]{1,0,4,3,2:T(2,128)(2,1)} %reshape.390), kind=kLoop, calls=%fused_computation.152 | loop fusion | bytes 9437184 | tf_op jit(solution)/shard_map/slice | solution.py:116
  116.8 9.1 %fusion.19 = (f32[12,512]{1,0:T(8,128)S(1)}, f32[12,512,512]{1,2,0:T(8,128)}) fusion(pred[512,512]{0,1:T(8,128)(4,1)S(1)} %fusion.47, bf16[1,512,1,12,64]{1,0,4,3,2:T(2,128)(2,1)} %get-tuple-element.71, bf16[1,512,1,12,64]{1,0,4,3,2:T(2,128)(2,1)} %get-tuple-element.72), kind=kOutput, calls=%fused_computation.39 | convolution fusion | flops 412084224 | bytes 14442496 | tf_op jit(solution)/shard_map/qhd,khd->hqk/dot_general | solution.py:42
  125.9 7.3 fusion.5
  133.3 5.9 fusion.44
  153.1 11.3 %multiply_convert_fusion.3 = (bf16[1024,3072]{1,0:T(8,128)(2,1)}, f32[1024,3072]{1,0:T(8,128)}) fusion(f32[3072]{0:T(1024)S(1)} %reshape.412, bf16[768,3840]{1,0:T(8,128)(2,1)S(1)} %copy-done.31, f32[1024,768]{0,1:T(8,128)S(1)} %get-tuple-element.106, f32[768]{0:T(1024)S(1)} %reshape.411, f32[768]{0:T(1024)S(1)} %reshape.410, ...), kind=kOutput, calls=%fused_computation.13 | convolution fusion | flops 4854644736 | bytes 26767360 | tf_op jit(solution)/shard_map/dot_general | solution.py:126
  164.4 48.5 %all-gather.8.cloned.1.call-done = bf16[3072,768]{1,0:T(8,128)(2,1)} async-done(((bf16[96,768]{1,0:T(8,128)(2,1)}), bf16[3072,768]{1,0:T(8,128)(2,1)}) %all-gather.8.cloned.1.call-update) | async-done | bytes 4718608 | tf_op jit(solution)/shard_map/all_gather | solution.py:108
  212.9 9.4 %fusion.78 = (f32[1024]{0:T(1024)S(1)}, f32[1024,768]{0,1:T(8,128)S(1)}) fusion(f32[768]{0:T(1024)S(1)} %reshape.413, bf16[1024,3072]{1,0:T(8,128)(2,1)} %get-tuple-element.107, bf16[3072,768]{1,0:T(8,128)(2,1)} %all-gather.8.cloned.1.call-done, f32[768]{0:T(1024)S(1)} %reshape.411, f32[768]{0:T(1024)S(1)} %reshape.410, f32[1024]{0:T(1024)S(1)} %add_rsqrt_fusion.1, ...), kind=kOutput, calls=%fused_computation.158 | convolution fusion | flops 4837342208 | bytes 17323008 | tf_op jit(solution)/shard_map/dot_general | solution.py:130
  228.8 16.2 %fusion.79 = (bf16[3072]{0:T(1024)(128)(2,1)}, bf16[1024,3072]{1,0:T(8,128)(2,1)}) fusion(f32[1024,3072]{1,0:T(8,128)} %get-tuple-element.108, f32[3072]{0:T(1024)S(1)} %reshape.412, bf16[1024,768]{0,1:T(8,128)(2,1)S(1)} %get-tuple-element.65, bf16[3072,768]{1,0:T(8,128)(2,1)S(1)} %bitcast.142), kind=kOutput, calls=%fused_computation.159 | convolution fusion | flops 4875875328 | bytes 25184256 | tf_op jit(solution)/shard_map/td,fd->tf/dot_general | solution.py:139
  245.1 11.4 %multiply_reduce_fusion.3 = (bf16[768]{0:T(1024)(128)(2,1)}, f32[1024]{0:T(1024)S(1)}, f32[1024]{0:T(1024)S(1)}, bf16[768]{0:T(1024)(128)(2,1)}, f32[1024,768]{0,1:T(8,128)S(1)}) fusion(f32[1024,768]{0,1:T(8,128)S(1)} %copy-done.3, f32[1024]{0:T(1024)S(1)} %add_rsqrt_fusion.1, f32[1024]{0:T(1024)S(1)} %broadcast_multiply_fusion.5, f32[768]{0:T(1024)S(1)} %reshape.410, ...), kind=kOutput, calls=%fused_computation.47 | convolution fusion | flops 4846776320 | bytes 22066176 | tf_op jit(solution)/shard_map/tf,df->td/dot_general | solution.py:143
  265.9 8.4 %multiply_reduce_fusion.1 = (f32[12,512]{1,0:T(8,128)S(1)}, f32[12,512,512]{1,2,0:T(8,128)}) fusion(f32[12,512]{1,0:T(8,128)S(1)} %log_add_fusion.1, f32[12,512,512]{1,2,0:T(8,128)S(1)} %bitcast.113, pred[512,512]{0,1:T(8,128)(4,1)S(1)} %fusion.47, bf16[512,12,64]{0,2,1:T(8,128)(2,1)S(1)} %bitcast.117, bf16[1,512,1,12,64]{1,0,4,3,2:T(2,128)(2,1)} %get-tuple-element.68), kind=kOutput, calls=%fused_computation.10 | convolution fusion | flops 418375680 | bytes 27049984 | tf_op jit(solution)/shard_map/qhd,khd->hqk/dot_general | solution.py:63
  274.3 10.0 %multiply_convert_fusion.1 = bf16[12,512,512]{1,2,0:T(8,128)(2,1)S(1)} fusion(f32[12,512,512]{1,2,0:T(8,128)} %get-tuple-element.115, f32[12,512]{1,0:T(8,128)S(1)} %get-tuple-element.114, f32[12,512]{1,0:T(8,128)S(1)} %log_add_fusion.1, f32[12,512,512]{1,2,0:T(8,128)} %get-tuple-element.104, pred[512,512]{0,1:T(8,128)(4,1)S(1)} %fusion.47), kind=kLoop, calls=%fused_computation.9 | loop fusion | flops 18874368 | bytes 31768576 | tf_op jit(solution)/shard_map/convert_element_type | solution.py:65
  290.8 7.1 multiply_reduce_fusion
  297.9 7.1 multiply_convert_fusion
  310.4 28.5 %fusion.18 = bf16[768,2304]{0,1:T(8,128)(2,1)S(1)} fusion(bf16[1024,768]{1,0:T(8,128)(2,1)S(1)} %copy-done.21, bf16[512,768]{0,1:T(8,128)(2,1)S(1)} %bitcast.134, bf16[512,768]{0,1:T(8,128)(2,1)S(1)} %bitcast.125, bf16[512,768]{0,1:T(8,128)(2,1)S(1)} %bitcast.128, bf16[512,768]{0,1:T(8,128)(2,1)S(1)} %bitcast.132, bf16[512,768]{0,1:T(8,128)(2,1)S(1)} %bitcast.119, ...), kind=kOutput, calls=%fused_computation.38 | convolution fusion | flops 3653959680 | bytes 9830400 | tf_op jit(solution)/shard_map/td,tc->dc/dot_general | solution.py:162
  362.8 10.0 %convolution_convert_fusion = bf16[3072,768]{1,0:T(8,128)(2,1)} fusion(bf16[1024,3072]{1,0:T(8,128)(2,1)} %get-tuple-element.107, bf16[1024,768]{0,1:T(8,128)(2,1)S(1)} %copy-done.23), kind=kOutput, calls=%fused_computation.33 | convolution fusion | flops 4834197504 | bytes 12582912 | tf_op jit(solution)/shard_map/tf,td->fd/dot_general | solution.py:137
  372.8 5.0 convolution_convert_fusion.4
  380.5 8.5 %convolution_convert_fusion.1 = bf16[768,3072]{1,0:T(8,128)(2,1)S(1)} fusion(bf16[1024,3072]{1,0:T(8,128)(2,1)} %get-tuple-element.117, f32[1024,768]{0,1:T(8,128)S(1)} %copy-done.4, f32[768]{0:T(1024)S(1)} %copy-done.29, f32[768]{0:T(1024)S(1)} %reshape.410, f32[1024]{0:T(1024)S(1)} %copy-done.27, f32[1024]{0:T(1024)S(1)} %broadcast_multiply_fusion.5), kind=kOutput, calls=%fused_computation.34 | convolution fusion | flops 4838129664 | bytes 14170112 | tf_op jit(solution)/shard_map/td,tf->df/dot_general | solution.py:142
  394.9 8.3 %fusion.32 = f32[1024,768]{0,1:T(8,128)S(1)} fusion(f32[1024,768]{0,1:T(8,128)} %copy-done.15, bf16[768,2432]{1,0:T(8,128)(2,1)} %all-gather.4.cloned.1.call-done, bf16[512,768]{0,1:T(8,128)(2,1)} %bitcast.135, bf16[512,768]{0,1:T(8,128)(2,1)} %bitcast.126, bf16[512,768]{0,1:T(8,128)(2,1)} %bitcast.129, bf16[512,768]{0,1:T(8,128)(2,1)} %bitcast.130, ...), kind=kOutput, calls=%fused_computation.71 | convolution fusion | flops 3652976640 | bytes 14548992 | tf_op jit(solution)/shard_map/tc,dc->td/dot_general | solution.py:172
  405.6 94.7 %all-reduce.5.cloned.1.call-done = bf16[768,2432]{0,1:T(8,128)(2,1)} async-done(((bf16[768,2432]{0,1:T(8,128)(2,1)}), bf16[768,2432]{0,1:T(8,128)(2,1)}) %all-reduce.5.cloned.1.call-update) | async-done | bytes 3735568
  505.6 106.8 %reduce-scatter.6.cloned.1.call-done = bf16[96,768]{1,0:T(8,128)(2,1)} async-done(((bf16[3072,768]{1,0:T(8,128)(2,1)}), bf16[96,768]{1,0:T(8,128)(2,1)}) %reduce-scatter.6.cloned.1.call-update) | async-done | bytes 147472 | tf_op jit(solution)/shard_map/reduce_scatter | solution.py:138
  614.1 116.2 %reduce-scatter.4.cloned.1.call-done = bf16[24,3840]{1,0:T(8,128)(2,1)} async-done(((bf16[768,3840]{1,0:T(8,128)(2,1)}), bf16[24,3840]{1,0:T(8,128)(2,1)}) %reduce-scatter.4.cloned.1.call-update) | async-done | bytes 184336 | tf_op jit(solution)/shard_map/reduce_scatter | solution.py:148
  (195 shorter events, 110.9 us)
Async XLA Ops:
  7.2 14.1 %copy-start.20 = (bf16[1024,768]{1,0:T(8,128)(2,1)S(1)}, bf16[1024,768]{1,0:T(8,128)(2,1)}, u32[]{:S(2)}) copy-start(bf16[1024,768]{1,0:T(8,128)(2,1)} %param.16) | copy-start | bytes 4718596
  7.2 15.7 %copy-start.30 = (s32[4,512]{1,0:T(4,128)S(1)}, s32[4,512]{1,0:T(4,128)}, u32[]{:S(2)}) copy-start(s32[4,512]{1,0:T(4,128)} %param.18) | copy-start | bytes 24580
  7.2 70.7 %all-gather.4.cloned.1.call-start = ((), (), s32[]{:S(2)}) async-start(), calls=%async_computation.2 | async-start | bytes 3852288 | tf_op jit(solution)/shard_map/all_gather | solution.py:92
  14.4 133.3 %all-gather.6.cloned.1.call-start = ((), (), s32[]{:S(2)}) async-start(), calls=%async_computation.3 | async-start | bytes 6082560 | tf_op jit(solution)/shard_map/all_gather | solution.py:103
  16.1 196.8 %all-gather.8.cloned.1.call-start = ((), (), s32[]{:S(2)}) async-start(), calls=%async_computation.4 | async-start | bytes 4866048 | tf_op jit(solution)/shard_map/all_gather | solution.py:108
  16.8 483.5 %all-reduce.5.cloned.1.call-start = ((), (), s32[]{:S(2)}) async-start(), calls=%async_computation.7 | async-start | bytes 7471104
  116.5 96.4 %copy-start.28 = (f32[768]{0:T(1024)}, f32[768]{0:T(1024)S(1)}, u32[]{:S(2)}) copy-start(f32[768]{0:T(1024)S(1)} %reshape.411) | copy-start | bytes 9220
  116.7 16.5 %slice-start = ((s8[12582912]{0:T(1024)(128)(4,1)}), s8[4194304]{0:T(1024)(128)(4,1)S(1)}, s32[]{:S(2)}) async-start(s8[12582912]{0:T(1024)(128)(4,1)} %bitcast.108), calls=%async_computation.8 | async-start | bytes 8388608
  116.8 16.5 %slice-start.1 = ((s8[12582912]{0:T(1024)(128)(4,1)}), s8[4194304]{0:T(1024)(128)(4,1)S(1)}, s32[]{:S(2)}) async-start(s8[12582912]{0:T(1024)(128)(4,1)} %bitcast.108), calls=%async_computation.9 | async-start | bytes 8388608
  153.1 103.3 %copy-start.26 = (f32[1024]{0:T(1024)}, f32[1024]{0:T(1024)S(1)}, u32[]{:S(2)}) copy-start(f32[1024]{0:T(1024)S(1)} %add_rsqrt_fusion.1) | copy-start | bytes 12292
  228.8 16.3 %copy-start.22 = (bf16[1024,768]{0,1:T(8,128)(2,1)}, bf16[1024,768]{0,1:T(8,128)(2,1)S(1)}, u32[]{:S(2)}) copy-start(bf16[1024,768]{0,1:T(8,128)(2,1)S(1)} %get-tuple-element.65) | copy-start | bytes 4718596
  228.8 16.3 %copy-start.3 = (f32[1024,768]{0,1:T(8,128)S(1)}, f32[1024,768]{0,1:T(8,128)}, u32[]{:S(2)}) copy-start(f32[1024,768]{0,1:T(8,128)} %copy-done.2) | copy-start | bytes 9437188
  228.8 33.1 %slice-start.6 = ((s8[12582912]{0:T(1024)(128)(4,1)}), s8[4194304]{0:T(1024)(128)(4,1)S(1)}, s32[]{:S(2)}) async-start(s8[12582912]{0:T(1024)(128)(4,1)} %bitcast.112), calls=%async_computation.14 | async-start | bytes 8388608
  228.8 33.1 %slice-start.7 = ((s8[12582912]{0:T(1024)(128)(4,1)}), s8[4194304]{0:T(1024)(128)(4,1)S(1)}, s32[]{:S(2)}) async-start(s8[12582912]{0:T(1024)(128)(4,1)} %bitcast.112), calls=%async_computation.15 | async-start | bytes 8388608
  245.1 16.8 %slice-start.8 = ((s8[12582912]{0:T(1024)(128)(4,1)}), s8[4194304]{0:T(1024)(128)(4,1)S(1)}, s32[]{:S(2)}) async-start(s8[12582912]{0:T(1024)(128)(4,1)} %bitcast.112), calls=%async_computation.16 | async-start | bytes 8388608
  265.9 21.7 %slice-start.3 = ((s8[12582912]{0:T(1024)(128)(4,1)}), s8[4194304]{0:T(1024)(128)(4,1)S(1)}, s32[]{:S(2)}) async-start(s8[12582912]{0:T(1024)(128)(4,1)} %bitcast.110), calls=%async_computation.11 | async-start | bytes 8388608
  265.9 21.7 %slice-start.4 = ((s8[12582912]{0:T(1024)(128)(4,1)}), s8[4194304]{0:T(1024)(128)(4,1)S(1)}, s32[]{:S(2)}) async-start(s8[12582912]{0:T(1024)(128)(4,1)} %bitcast.110), calls=%async_computation.12 | async-start | bytes 8388608
  274.3 13.3 %slice-start.5 = ((s8[12582912]{0:T(1024)(128)(4,1)}), s8[4194304]{0:T(1024)(128)(4,1)S(1)}, s32[]{:S(2)}) async-start(s8[12582912]{0:T(1024)(128)(4,1)} %bitcast.110), calls=%async_computation.13 | async-start | bytes 8388608
  286.4 24.0 %copy-start.16 = (bf16[12,64,512]{2,1,0:T(8,128)(2,1)}, bf16[12,64,512]{2,1,0:T(8,128)(2,1)S(1)}, u32[]{:S(2)}) copy-start(bf16[12,64,512]{2,1,0:T(8,128)(2,1)S(1)} %multiply_convert_fusion.7) | copy-start | bytes 2359300
  287.5 22.9 %copy-start.17 = (bf16[12,64,512]{2,1,0:T(8,128)(2,1)}, bf16[12,64,512]{2,1,0:T(8,128)(2,1)S(1)}, u32[]{:S(2)}) copy-start(bf16[12,64,512]{2,1,0:T(8,128)(2,1)S(1)} %multiply_convert_fusion.8) | copy-start | bytes 2359300
  290.8 19.6 %copy-start.25 = (bf16[12,64,512]{2,1,0:T(8,128)(2,1)}, bf16[12,64,512]{2,1,0:T(8,128)(2,1)S(1)}, u32[]{:S(2)}) copy-start(bf16[12,64,512]{2,1,0:T(8,128)(2,1)S(1)} %fusion.41) | copy-start | bytes 2359300
  308.2 30.8 %copy-start.19 = (bf16[12,64,512]{2,1,0:T(8,128)(2,1)}, bf16[12,64,512]{2,1,0:T(8,128)(2,1)S(1)}, u32[]{:S(2)}) copy-start(bf16[12,64,512]{2,1,0:T(8,128)(2,1)S(1)} %multiply_convert_fusion.6) | copy-start | bytes 2359300
  361.4 251.1 %reduce-scatter.6.cloned.1.call-start = ((), (), s32[]{:S(2)}) async-start(), calls=%async_computation.6 | async-start | bytes 4866048 | tf_op jit(solution)/shard_map/reduce_scatter | solution.py:138
  372.8 357.5 %reduce-scatter.4.cloned.1.call-start = ((), (), s32[]{:S(2)}) async-start(), calls=%async_computation.5 | async-start | bytes 6082560 | tf_op jit(solution)/shard_map/reduce_scatter | solution.py:148
  (26 other events, 125.6 us)
Sparse Core Ops, SparseCore 0:
  14.5 63.3 all-gather.3
  81.3 66.3 all-gather.5
  150.6 62.2 all-gather.7
  361.5 138.7 all-reduce.4
  505.6 106.7 reduce-scatter.5
  617.9 112.3 reduce-scatter.3
